TPU v7x, 32 devices: a whole 2x2x4 slice. The times are simulated.
32 devices in a mesh: cell: 16 (over z, y, x), win: 2 (over core).
Axes of the slice: x: 2, y: 2, z: 4, core: 2. Of those that a mesh axis runs over, the one named last changes fastest.
Arguments:
- anomalies: bfloat16 [256, 60, 8192], P('win', None, 'cell'), may hold values from -6 to 6
- eofs: bfloat16 [100, 60, 8192], P('win', None, 'cell'), may hold values from -0.015625 to 0.015625
- cell_area: float32 [8192], P('cell'), may hold values from 0.5 to 2
- levels: int32 [8192], P('cell'), may hold values from 1 to 60
- counts: int32 [16], replicated, may hold values from 128 to 512, as said below
Outputs:
- pcs: float32 [256, 100], P('win')
- regression: float32 [100, 8192], P('win', 'cell')
Inputs may be any that keep to these rules, and one draw needn't show every extreme that they name: `counts`: every entry is at most 512, and some block holds exactly 512 real cells.
All inputs are finite; a program needn't handle non-finite values.
Results may differ from a plain program's by a relative error of at most 0.0049.
Values may be sent and summed in bfloat16 or wider, within the bound.
No kernel may reach another device: no remote copies, remote signals or barrier semaphores. Data moves between devices by JAX's collectives and lax.ppermute only.
A program may use at most 64 MiB of HBM per device.

v0:
```python
import jax
import jax.numpy as jnp
from jax import lax
from jax.sharding import PartitionSpec as P


def shards(anomalies, eofs, cell_area, levels, counts):
    steps_here, depth_count, slots = anomalies.shape
    position = lax.axis_index("cell")
    filled = counts[position]
    live = jnp.arange(slots, dtype=jnp.int32) < filled
    depth = jnp.arange(depth_count, dtype=jnp.int32)[:, None] < levels[None, :]
    mask = (live[None, :] & depth).astype(jnp.float32)
    weighted = (eofs.astype(jnp.float32) * (cell_area[None, :] * mask)[None]).astype(jnp.bfloat16)
    flat_data = anomalies.reshape(steps_here, depth_count * slots)
    piece = lax.all_gather(weighted, "win", axis=0, tiled=True)
    flat_piece = piece.reshape(piece.shape[0], depth_count * slots)
    partial_value = lax.dot_general(
        flat_data, flat_piece, (((1,), (1,)), ((), ())), preferred_element_type=jnp.float32
    )
    pcs = lax.psum(partial_value, "cell")
    column = jnp.sum(anomalies.astype(jnp.float32) * mask[None], axis=1).astype(jnp.bfloat16)
    pcs_rounded = pcs.astype(jnp.bfloat16)
    windows = lax.axis_size("win")
    term = lax.dot_general(
        pcs_rounded, column, (((0,), (0,)), ((), ())), preferred_element_type=jnp.float32
    )
    term = term / jnp.sqrt(jnp.float32(steps_here * windows))
    regression = lax.psum_scatter(term, "win", scatter_dimension=0, tiled=True)
    return (pcs, regression)


def solution(mesh):
    in_specs = (P("win", None, "cell"), P("win", None, "cell"), P("cell"), P("cell"), P())
    out_specs = (P("win", None), P("win", "cell"))
    return jax.shard_map(shards, mesh=mesh, in_specs=in_specs, out_specs=out_specs, check_vma=False)
```

profile of v0, /device:TPU:0, one launch (start us, length us, event | category | flops | bytes accessed | tf_op | source)
XLA Modules:
  0.0 138.4 jit_solution(9140950876646721835)
XLA Ops:
  7.2 0.0 copy-start.1
  7.2 0.0 all-gather.2.cloned.1.call-start
  7.2 1.2 dynamic_slice.3
  8.5 0.6 iota_compare_fusion.1
  9.1 0.7 fusion.9
  9.9 4.6 %multiply_convert_fusion = bf16[50,60,512]{2,1,0:T(8,128)(2,1)} fusion(bf16[50,60,512]{2,1,0:T(8,128)(2,1)} %param.6, f32[60,512]{1,0:T(8,128)S(1)} %fusion.9), kind=kLoop, calls=%fused_computation.1 | loop fusion | flops 4608000 | bytes 6266880 | tf_op jit(solution)/shard_map/convert_element_type | solution.py:14
  14.5 0.0 all-gather.2.cloned.1.call-update
  14.5 0.0 copy-done.1
  14.5 5.0 %multiply_reduce_fusion = bf16[128,512]{1,0:T(8,128)(2,1)S(1)} fusion(bf16[128,60,512]{2,0,1:T(8,128)(2,1)} %param.5, f32[60,512]{1,0:T(8,128)S(1)} %fusion.8), kind=kLoop, calls=%fused_computation | loop fusion | flops 11730944 | bytes 8118272 | tf_op jit(solution)/shard_map/reduce_sum | solution.py:22
  19.5 0.0 copy-start.2
  19.5 15.0 %all-gather.2.cloned.1.call-done = bf16[100,60,512]{2,1,0:T(8,128)(2,1)} async-done(((bf16[50,60,512]{2,1,0:T(8,128)(2,1)}), bf16[100,60,512]{2,1,0:T(8,128)(2,1)}) %all-gather.2.cloned.1.call-update) | async-done | bytes 6144016 | tf_op jit(solution)/shard_map/all_gather | solution.py:16
  34.5 12.3 %fusion.3 = f32[128,100]{0,1:T(8,128)S(1)} fusion(bf16[128,60,512]{2,0,1:T(8,128)(2,1)} %param.5, bf16[100,60,512]{2,1,0:T(8,128)(2,1)} %all-gather.2.cloned.1.call-done), kind=kOutput, calls=%fused_computation.5 | convolution fusion | flops 786432000 | bytes 14059520 | tf_op jit(solution)/shard_map/dot_general | solution.py:18
  46.8 77.1 %psum.7 = f32[128,100]{0,1:T(8,128)S(1)} all-reduce(f32[128,100]{0,1:T(8,128)S(1)} %fusion.3), channel_id=1, replica_groups=mesh['cell'=16,'win'=2] {'cell'}, use_global_device_ids=true, to_apply=%region_0.0 | all-reduce | flops 12800 | bytes 102400 | tf_op jit(solution)/shard_map/psum | solution.py:21
  123.9 0.0 copy-start
  123.9 0.2 convolution_multiply_fusion
  124.1 3.1 %fusion = f32[56,512]{1,0:T(8,128)S(1)} fusion(f32[100,512]{1,0:T(8,128)S(1)} %convolution_multiply_fusion), kind=kCustom, calls=%all-reduce-scatter | all-reduce-scatter fusion | flops 57345 | bytes 320000
  127.1 2.3 %collective-permute-start = (f32[6,512]{1,0:T(8,128)S(1)}, f32[6,512]{1,0:T(8,128)S(1)}, u32[]{:S(2)}, u32[]{:S(2)}) collective-permute-start(f32[6,512]{1,0:T(8,128)S(1)} %slice), channel_id=1, source_target_pairs={{0,1},{2,3},{4,5},{6,7},{8,9},{10,11},{12,13},{14,15},{16,17},{18,... | collective-permute-start | bytes 36872
  129.4 0.0 copy-done.2
  129.4 0.6 dynamic-slice.4
  130.7 0.0 collective-permute-done
  130.7 0.2 concatenate
  130.9 0.7 constant_dynamic-slice_fusion
  131.5 0.0 copy-done
  (2 shorter events, 0.0 us)
Async XLA Ops:
  7.2 7.3 %copy-start.1 = (s32[512]{0:T(512)S(1)}, s32[512]{0:T(512)}, u32[]{:S(2)}) copy-start(s32[512]{0:T(512)} %param.8) | copy-start | bytes 6148
  7.2 27.3 %all-gather.2.cloned.1.call-start = ((), (), s32[]{:S(2)}) async-start(), calls=%async_computation | async-start | bytes 9830400 | tf_op jit(solution)/shard_map/all_gather | solution.py:16
  19.5 109.9 %copy-start.2 = (u32[32]{0:T(128)S(1)}, u32[32]{0:T(128)}, u32[]{:S(2)}) copy-start(u32[32]{0:T(128)} %constant.18) | copy-start | bytes 388
  123.9 7.6 %copy-start = (f32[128,100]{0,1:T(8,128)}, f32[128,100]{0,1:T(8,128)S(1)}, u32[]{:S(2)}) copy-start(f32[128,100]{0,1:T(8,128)S(1)} %psum.7) | copy-start | bytes 153604
  127.1 3.5 %collective-permute-start = (f32[6,512]{1,0:T(8,128)S(1)}, f32[6,512]{1,0:T(8,128)S(1)}, u32[]{:S(2)}, u32[]{:S(2)}) collective-permute-start(f32[6,512]{1,0:T(8,128)S(1)} %slice), channel_id=1, source_target_pairs={{0,1},{2,3},{4,5},{6,7},{8,9},{10,11},{12,13},{14,15},{16,17},{18,... | collective-permute-start | bytes 36872
Sparse Core Ops, SparseCore 0:
  14.6 19.8 all-gather.1
where the time goes:
time: 139 us; the launch traced here: 138 us
  blocking collectives  80.2 us (58%)
  waiting for transfers between devices  15 us (11%)
  between operations  14.8 us (11%)
  matrix products  12.4 us (9%)
  other arithmetic  11 us (8%)
  local copies, waits for them, and re-layouts  2.69 us (2%)
  starting transfers between devices  2.3 us (2%)
    psum x1, blocking collectives, shards(): pcs = lax.psum(partial_value, 'cell')  77.1 us
    all_gather x1, waiting for transfers between devices, shards(): piece = lax.all_gather(weighted, 'win', axis=0, tiled=True)  15 us
    dot_general x1, matrix products, shards(): lax.dot_general(flat_data, flat_piece, (((1,), (1,)), ((), ())), preferre...  12.3 us
    reduce_sum x1, other arithmetic, shards(): jnp.sum(anomalies.astype(jnp.float32) * mask[None], axis=1)  5.01 us
    convert_element_type x1, other arithmetic, shards(): (eofs.astype(jnp.float32) * (cell_area[None, :] * mask)[None]).astype(jnp...  4.6 us
    unnamed x1, blocking collectives  3.06 us
  transfers between devices with their start and end apart: 2, of which 1 were waited for; matrix products, arithmetic and copies ran while one was open for 4% of the time, Pallas kernels for 0%

commit v1 on v0

--- a/solution.py
+++ b/solution.py
@@ -18,7 +18,9 @@
     partial_value = lax.dot_general(
         flat_data, flat_piece, (((1,), (1,)), ((), ())), preferred_element_type=jnp.float32
     )
-    pcs = lax.psum(partial_value, "cell")
+    pcs = partial_value
+    for hop in (1, 2, 4, 8):
+        pcs = pcs + lax.ppermute(pcs, "cell", [(dev, dev ^ hop) for dev in range(16)])
     column = jnp.sum(anomalies.astype(jnp.float32) * mask[None], axis=1).astype(jnp.bfloat16)
     pcs_rounded = pcs.astype(jnp.bfloat16)
     windows = lax.axis_size("win")

time: 139 us -> 82.5 us (0.59)
  blocking collectives: 80.2 us -> 3.06 us
  waiting for transfers between devices: 15 us -> 27.2 us
  starting transfers between devices: 2.3 us -> 11 us
    psum x1 -> x0, blocking collectives: 77.1 us -> none  [shards(): pcs = lax.psum(partial_value, 'cell')]
    ppermute x0 -> x4, starting transfers between devices: none -> 8.68 us  [shards(): lax.ppermute(pcs, 'cell', [(dev, dev ^ hop) for dev in range(16)])]
    ppermute x0 -> x4, waiting for transfers between devices: none -> 7.14 us  [shards(): lax.ppermute(pcs, 'cell', [(dev, dev ^ hop) for dev in range(16)])]
    all_gather x1, waiting for transfers between devices: 15 us -> 20 us  [shards(): piece = lax.all_gather(weighted, 'win', axis=0, tiled=True)]
  transfers between devices with their start and end apart: 2 -> 6, of which waited for: 1 -> 4; matrix products, arithmetic and copies ran while one was open for 4% -> 7% of each run, Pallas kernels for 0% -> 0%
where the time goes in v1:
time: 82.5 us; the launch traced here: 82.2 us
  waiting for transfers between devices  27.2 us (33%)
  between operations  14.8 us (18%)
  matrix products  12.4 us (15%)
  starting transfers between devices  11 us (13%)
  other arithmetic  11 us (13%)
  blocking collectives  3.06 us (4%)
  local copies, waits for them, and re-layouts  2.69 us (3%)
    all_gather x1, waiting for transfers between devices, shards(): piece = lax.all_gather(weighted, 'win', axis=0, tiled=True)  20 us
    dot_general x1, matrix products, shards(): lax.dot_general(flat_data, flat_piece, (((1,), (1,)), ((), ())), preferre...  12.3 us
    ppermute x4, starting transfers between devices, shards(): lax.ppermute(pcs, 'cell', [(dev, dev ^ hop) for dev in range(16)])  8.68 us
    ppermute x4, waiting for transfers between devices, shards(): lax.ppermute(pcs, 'cell', [(dev, dev ^ hop) for dev in range(16)])  7.14 us
    reduce_sum x1, other arithmetic, shards(): jnp.sum(anomalies.astype(jnp.float32) * mask[None], axis=1)  5 us
    convert_element_type x1, other arithmetic, shards(): (eofs.astype(jnp.float32) * (cell_area[None, :] * mask)[None]).astype(jnp...  4.6 us
    unnamed x1, blocking collectives  3.06 us
    unnamed x1, starting transfers between devices  2.26 us
  transfers between devices with their start and end apart: 6, of which 4 were waited for; matrix products, arithmetic and copies ran while one was open for 7% of the time, Pallas kernels for 0%

profile of v1, /device:TPU:0, one launch (start us, length us, event | category | flops | bytes accessed | tf_op | source)
XLA Modules:
  0.0 82.2 jit_solution(15157126811846779050)
XLA Ops:
  7.2 0.0 all-gather.2.cloned.1.call-start
  7.2 1.2 %dynamic_slice.3 = s32[1]{0:T(128)} dynamic-slice(s32[16]{0:T(128)} %param.9, s32[]{:T(128)S(6)} %select_n.3), dynamic_slice_sizes={1} | dynamic-slice | bytes 12 | tf_op jit(solution)/shard_map/dynamic_slice | solution.py:10
  8.5 0.6 iota_compare_fusion.1
  9.1 0.7 fusion.9
  9.8 4.6 %multiply_convert_fusion = bf16[50,60,512]{2,1,0:T(8,128)(2,1)} fusion(bf16[50,60,512]{2,1,0:T(8,128)(2,1)} %param.6, f32[60,512]{1,0:T(8,128)S(1)} %fusion.9), kind=kLoop, calls=%fused_computation.1 | loop fusion | flops 4608000 | bytes 6266880 | tf_op jit(solution)/shard_map/convert_element_type | solution.py:14
  14.4 0.0 all-gather.2.cloned.1.call-update
  14.5 0.0 copy-start.1
  14.5 20.0 %all-gather.2.cloned.1.call-done = bf16[100,60,512]{2,1,0:T(8,128)(2,1)} async-done(((bf16[50,60,512]{2,1,0:T(8,128)(2,1)}), bf16[100,60,512]{2,1,0:T(8,128)(2,1)}) %all-gather.2.cloned.1.call-update) | async-done | bytes 6144016 | tf_op jit(solution)/shard_map/all_gather | solution.py:16
  34.5 12.3 %fusion.3 = f32[128,100]{0,1:T(8,128)S(1)} fusion(bf16[128,60,512]{2,0,1:T(8,128)(2,1)} %param.5, bf16[100,60,512]{2,1,0:T(8,128)(2,1)} %all-gather.2.cloned.1.call-done), kind=kOutput, calls=%fused_computation.5 | convolution fusion | flops 786432000 | bytes 14059520 | tf_op jit(solution)/shard_map/dot_general | solution.py:18
  46.8 0.0 copy-start.2
  46.8 1.8 %collective-permute-start = (f32[128,100]{0,1:T(8,128)S(1)}, f32[128,100]{0,1:T(8,128)S(1)}, u32[]{:S(2)}, u32[]{:S(2)}) collective-permute-start(f32[128,100]{0,1:T(8,128)S(1)} %fusion.3), channel_id=1, source_target_pairs={{0,2},{2,0},{4,6},{6,4},{8,10},{10,8},{12,14},{14,12},{16,18},{18,... | collective-permute-start | bytes 153608 | tf_op jit(solution)/shard_map/ppermute | solution.py:23
  48.6 2.4 %collective-permute-done = f32[128,100]{0,1:T(8,128)S(1)} collective-permute-done((f32[128,100]{0,1:T(8,128)S(1)}, f32[128,100]{0,1:T(8,128)S(1)}, u32[]{:S(2)}, u32[]{:S(2)}) %collective-permute-start) | collective-permute-done | bytes 51232 | tf_op jit(solution)/shard_map/ppermute | solution.py:23
  51.0 1.8 %collective-permute-start.1 = (f32[128,100]{0,1:T(8,128)S(1)}, f32[128,100]{0,1:T(8,128)S(1)}, u32[]{:S(2)}, u32[]{:S(2)}) collective-permute-start(f32[128,100]{0,1:T(8,128)S(1)} %add.18), channel_id=1, source_target_pairs={{0,4},{2,6},{4,0},{6,2},{8,12},{10,14},{12,8},{14,10},{16,20},{18,... | collective-permute-start | bytes 153608 | tf_op jit(solution)/shard_map/ppermute | solution.py:23
  52.8 2.4 %collective-permute-done.1 = f32[128,100]{0,1:T(8,128)S(1)} collective-permute-done((f32[128,100]{0,1:T(8,128)S(1)}, f32[128,100]{0,1:T(8,128)S(1)}, u32[]{:S(2)}, u32[]{:S(2)}) %collective-permute-start.1) | collective-permute-done | bytes 51232 | tf_op jit(solution)/shard_map/ppermute | solution.py:23
  55.2 1.8 %collective-permute-start.2 = (f32[128,100]{0,1:T(8,128)S(1)}, f32[128,100]{0,1:T(8,128)S(1)}, u32[]{:S(2)}, u32[]{:S(2)}) collective-permute-start(f32[128,100]{0,1:T(8,128)S(1)} %add.19), channel_id=1, source_target_pairs={{0,8},{2,10},{4,12},{6,14},{8,0},{10,2},{12,4},{14,6},{16,24},{18,... | collective-permute-start | bytes 153608 | tf_op jit(solution)/shard_map/ppermute | solution.py:23
  57.0 0.0 copy-done.1
  57.0 2.4 %collective-permute-done.2 = f32[128,100]{0,1:T(8,128)S(1)} collective-permute-done((f32[128,100]{0,1:T(8,128)S(1)}, f32[128,100]{0,1:T(8,128)S(1)}, u32[]{:S(2)}, u32[]{:S(2)}) %collective-permute-start.2) | collective-permute-done | bytes 51232 | tf_op jit(solution)/shard_map/ppermute | solution.py:23
  59.4 3.3 %collective-permute-start.3 = (f32[128,100]{0,1:T(8,128)S(1)}, f32[128,100]{0,1:T(8,128)S(1)}, u32[]{:S(2)}, u32[]{:S(2)}) collective-permute-start(f32[128,100]{0,1:T(8,128)S(1)} %add.20), channel_id=1, source_target_pairs={{0,16},{2,18},{4,20},{6,22},{8,24},{10,26},{12,28},{14,30},{16,0},... | collective-permute-start | bytes 153608 | tf_op jit(solution)/shard_map/ppermute | solution.py:23
  62.7 5.0 %multiply_reduce_fusion = bf16[128,512]{1,0:T(8,128)(2,1)S(1)} fusion(bf16[128,60,512]{2,0,1:T(8,128)(2,1)} %param.5, f32[60,512]{1,0:T(8,128)S(1)} %fusion.8), kind=kLoop, calls=%fused_computation | loop fusion | flops 11730944 | bytes 8118272 | tf_op jit(solution)/shard_map/reduce_sum | solution.py:24
  67.7 0.0 collective-permute-done.3
  67.7 0.0 copy-start
  67.7 0.2 convolution_multiply_fusion
  67.9 3.1 %fusion = f32[56,512]{1,0:T(8,128)S(1)} fusion(f32[100,512]{1,0:T(8,128)S(1)} %convolution_multiply_fusion), kind=kCustom, calls=%all-reduce-scatter | all-reduce-scatter fusion | flops 57345 | bytes 320000
  71.0 2.3 %collective-permute-start.4 = (f32[6,512]{1,0:T(8,128)S(1)}, f32[6,512]{1,0:T(8,128)S(1)}, u32[]{:S(2)}, u32[]{:S(2)}) collective-permute-start(f32[6,512]{1,0:T(8,128)S(1)} %slice), channel_id=1, source_target_pairs={{0,1},{2,3},{4,5},{6,7},{8,9},{10,11},{12,13},{14,15},{16,17},{18,... | collective-permute-start | bytes 36872
  73.2 0.0 copy-done.2
  73.2 0.6 dynamic-slice.4
  74.5 0.0 collective-permute-done.4
  74.5 0.2 concatenate
  74.7 0.7 constant_dynamic-slice_fusion
  75.3 0.0 copy-done
  (6 shorter events, 0.1 us)
Async XLA Ops:
  7.2 27.3 %all-gather.2.cloned.1.call-start = ((), (), s32[]{:S(2)}) async-start(), calls=%async_computation | async-start | bytes 9830400 | tf_op jit(solution)/shard_map/all_gather | solution.py:16
  14.5 42.5 %copy-start.1 = (s32[512]{0:T(512)S(1)}, s32[512]{0:T(512)}, u32[]{:S(2)}) copy-start(s32[512]{0:T(512)} %param.8) | copy-start | bytes 6148
  46.8 26.5 %copy-start.2 = (u32[32]{0:T(128)S(1)}, u32[32]{0:T(128)}, u32[]{:S(2)}) copy-start(u32[32]{0:T(128)} %constant.18) | copy-start | bytes 388
  46.8 4.2 %collective-permute-start = (f32[128,100]{0,1:T(8,128)S(1)}, f32[128,100]{0,1:T(8,128)S(1)}, u32[]{:S(2)}, u32[]{:S(2)}) collective-permute-start(f32[128,100]{0,1:T(8,128)S(1)} %fusion.3), channel_id=1, source_target_pairs={{0,2},{2,0},{4,6},{6,4},{8,10},{10,8},{12,14},{14,12},{16,18},{18,... | collective-permute-start | bytes 153608 | tf_op jit(solution)/shard_map/ppermute | solution.py:23
  51.0 4.2 %collective-permute-start.1 = (f32[128,100]{0,1:T(8,128)S(1)}, f32[128,100]{0,1:T(8,128)S(1)}, u32[]{:S(2)}, u32[]{:S(2)}) collective-permute-start(f32[128,100]{0,1:T(8,128)S(1)} %add.18), channel_id=1, source_target_pairs={{0,4},{2,6},{4,0},{6,2},{8,12},{10,14},{12,8},{14,10},{16,20},{18,... | collective-permute-start | bytes 153608 | tf_op jit(solution)/shard_map/ppermute | solution.py:23
  55.2 4.2 %collective-permute-start.2 = (f32[128,100]{0,1:T(8,128)S(1)}, f32[128,100]{0,1:T(8,128)S(1)}, u32[]{:S(2)}, u32[]{:S(2)}) collective-permute-start(f32[128,100]{0,1:T(8,128)S(1)} %add.19), channel_id=1, source_target_pairs={{0,8},{2,10},{4,12},{6,14},{8,0},{10,2},{12,4},{14,6},{16,24},{18,... | collective-permute-start | bytes 153608 | tf_op jit(solution)/shard_map/ppermute | solution.py:23
  59.4 8.3 %collective-permute-start.3 = (f32[128,100]{0,1:T(8,128)S(1)}, f32[128,100]{0,1:T(8,128)S(1)}, u32[]{:S(2)}, u32[]{:S(2)}) collective-permute-start(f32[128,100]{0,1:T(8,128)S(1)} %add.20), channel_id=1, source_target_pairs={{0,16},{2,18},{4,20},{6,22},{8,24},{10,26},{12,28},{14,30},{16,0},... | collective-permute-start | bytes 153608 | tf_op jit(solution)/shard_map/ppermute | solution.py:23
  67.7 7.6 %copy-start = (f32[128,100]{0,1:T(8,128)}, f32[128,100]{0,1:T(8,128)S(1)}, u32[]{:S(2)}) copy-start(f32[128,100]{0,1:T(8,128)S(1)} %add.21) | copy-start | bytes 153604
  71.0 3.5 %collective-permute-start.4 = (f32[6,512]{1,0:T(8,128)S(1)}, f32[6,512]{1,0:T(8,128)S(1)}, u32[]{:S(2)}, u32[]{:S(2)}) collective-permute-start(f32[6,512]{1,0:T(8,128)S(1)} %slice), channel_id=1, source_target_pairs={{0,1},{2,3},{4,5},{6,7},{8,9},{10,11},{12,13},{14,15},{16,17},{18,... | collective-permute-start | bytes 36872
Sparse Core Ops, SparseCore 0:
  14.6 19.8 all-gather.1
